TPU v7x, 32 devices: a whole 2x2x4 slice. The times are simulated.
32 devices in a mesh: depth: 4 (over y, x), chan: 8 (over z, core).
Axes of the slice: x: 2, y: 2, z: 4, core: 2. Of those that a mesh axis runs over, the one named last changes fastest.
Arguments:
- volume: float32 [512, 16, 1024], P('chan', 'depth'), may hold values from -6 to 6
- conv_weight: float32 [1, 3, 16, 32, 864], P(None, None, 'chan'), may hold values from -0.21875 to 0.21875
- norm_gain: float32 [1, 512], replicated, may hold values from 0.1 to 1.9
- mlp_in: float32 [1, 1024, 512], replicated, may hold values from -0.25 to 0.25
- mlp_out: float32 [1, 512, 1024], replicated, may hold values from -0.1875 to 0.1875
Outputs:
- features: float32 [512, 16, 1024], P('chan', 'depth')
All inputs are finite; a program needn't handle non-finite values.
Results may differ from a plain program's by a relative error of at most 0.0001.
Values sent between devices are 32-bit elements; how exact they have to be, the bound alone decides.
A program may use at most 64 MiB of HBM per device.

v0:
```python
import functools

import jax
import jax.numpy as jnp
from jax import lax
from jax.experimental import pallas as pl
from jax.experimental.pallas import tpu as pltpu
from jax.sharding import PartitionSpec as P

W = 32
LIMIT = 60 * 1024 * 1024


def split(x):
    hi = x.astype(jnp.bfloat16)
    return hi, (x - hi.astype(jnp.float32)).astype(jnp.bfloat16)


def dot3(a, b):
    a_hi, a_lo = a
    b_hi, b_lo = b
    dot = functools.partial(jnp.dot, preferred_element_type=jnp.float32)
    return dot(a_hi, b_hi) + (dot(a_hi, b_lo) + dot(a_lo, b_hi))


def conv_body(last, chunk, *refs):
    if last:
        own, up, down, res, w, out, wf, wb, xb, acc = refs
    else:
        own, up, down, w, out, wf, wb, xb, acc = refs
        res = None
    planes, width, cells = own.shape
    deep = (planes + 2) * width
    span = 3 * deep

    @pl.when(pl.program_id(0) == 0)
    def _():
        wf[...] = jnp.zeros_like(wf)

    for b in range(3):
        for c in range(3):
            start = (b * 3 + c) * 3 * width
            piece = w[0, :, start : start + 3 * width]
            hi = piece.astype(jnp.bfloat16).astype(jnp.float32)
            lo = piece - hi
            for z in range(planes):
                row = (b * planes + z) * width
                for part, value in enumerate((hi, hi, lo)):
                    col = part * span + c * deep + z * width
                    wf[row : row + width, col : col + 3 * width] = value
    wb[...] = wf[...].astype(jnp.bfloat16)

    column = lax.broadcasted_iota(jnp.int32, (width, cells), 1) % W
    for z in range(planes + 2):
        x = up[0] if z == 0 else down[0] if z == planes + 1 else own[z - 1]
        before = jnp.where(column == 0, pltpu.roll(x, cells + 1 - W, 1), pltpu.roll(x, 1, 1))
        after = jnp.where(column == W - 1, pltpu.roll(x, W - 1, 1), pltpu.roll(x, cells - 1, 1))
        for c, value in enumerate((before, x, after)):
            hi, lo = split(value)
            row = c * deep + z * width
            xb[row : row + width, :] = hi
            xb[span + row : span + row + width, :] = lo
            xb[2 * span + row : 2 * span + row + width, :] = hi

    step = min(256, cells)
    for n in range(0, cells, step):
        acc[:, n : n + step] = jnp.dot(
            wb[...], xb[:, n : n + step], preferred_element_type=jnp.float32
        )

    for z in range(planes):
        p0, p1, p2 = (acc[(b * planes + z) * width : (b * planes + z + 1) * width, :] for b in range(3))
        value = p1 + pltpu.roll(p0, W, 1) + pltpu.roll(p2, cells - W, 1)
        if last:
            value = value + res[z]
            per = cells // chunk
            for q in range(per):
                out[z * per + q] = value[:, q * chunk : (q + 1) * chunk]
        else:
            out[z] = jax.nn.gelu(value)


def conv(own, up, down, kernel, res=None, chunk=None):
    planes, channels, cells = own.shape
    groups, width, taps = kernel.shape
    last = res is not None
    rows = 3 * planes * width
    span = 9 * (planes + 2) * width
    slab = pl.BlockSpec((planes, width, cells), lambda g: (0, g, 0))
    edge = pl.BlockSpec((1, width, cells), lambda g: (0, g, 0))
    weights = pl.BlockSpec((1, width, taps), lambda g: (g, 0, 0))
    if last:
        parts = planes * cells // chunk
        out_shape = (parts, channels, chunk)
        out_spec = pl.BlockSpec((parts, width, chunk), lambda g: (0, g, 0))
        args, specs = (own, up, down, res, kernel), [slab, edge, edge, slab, weights]
    else:
        out_shape, out_spec = own.shape, slab
        args, specs = (own, up, down, kernel), [slab, edge, edge, weights]
    return pl.pallas_call(
        functools.partial(conv_body, last, chunk),
        grid=(groups,),
        in_specs=specs,
        out_specs=out_spec,
        out_shape=jax.ShapeDtypeStruct(out_shape, jnp.float32),
        scratch_shapes=[
            pltpu.VMEM((rows, span), jnp.float32),
            pltpu.VMEM((rows, span), jnp.bfloat16),
            pltpu.VMEM((span, cells), jnp.bfloat16),
            pltpu.VMEM((rows, cells), jnp.float32),
        ],
        compiler_params=pltpu.CompilerParams(vmem_limit_bytes=LIMIT),
        name="conv",
    )(*args)


def mlp_body(x_ref, gain, w_in, w_out, out, r_hi, r_lo):
    @pl.when(pl.program_id(0) == 0)
    def _():
        x = x_ref[...]
        r = x * lax.rsqrt(jnp.mean(x * x, axis=0, keepdims=True) + 1e-06) * gain[...]
        hi, lo = split(r)
        r_hi[...] = hi
        r_lo[...] = lo
        out[...] = x

    hidden = jax.nn.gelu(dot3(split(w_in[...]), (r_hi[...], r_lo[...])))
    out[...] += dot3(split(w_out[...]), split(hidden))


def mlp(x, gain, w_in, w_out):
    channels, cells = x.shape
    hid = w_in.shape[0]
    block = min(256, hid)
    whole = pl.BlockSpec((channels, cells), lambda k: (0, 0))
    return pl.pallas_call(
        mlp_body,
        grid=(hid // block,),
        in_specs=[
            whole,
            pl.BlockSpec((channels, 1), lambda k: (0, 0)),
            pl.BlockSpec((block, channels), lambda k: (k, 0)),
            pl.BlockSpec((channels, block), lambda k: (0, k)),
        ],
        out_specs=whole,
        out_shape=jax.ShapeDtypeStruct(x.shape, jnp.float32),
        scratch_shapes=[pltpu.VMEM(x.shape, jnp.bfloat16)] * 2,
        compiler_params=pltpu.CompilerParams(vmem_limit_bytes=LIMIT),
        name="mlp",
    )(x, gain.reshape(-1, 1), w_in, w_out)


def exchange_body(count, src, out, send_sem, recv_sem, own_sem):
    me = lax.axis_index("chan")
    barrier = pltpu.get_barrier_semaphore()
    for k in range(1, count):
        pl.semaphore_signal(
            barrier,
            inc=1,
            device_id={"chan": lax.rem(me + k, count)},
            device_id_type=pl.DeviceIdType.MESH,
        )
    own = pltpu.make_async_copy(src.at[me], out.at[me], own_sem)
    own.start()
    pl.semaphore_wait(barrier, count - 1)
    copies = []
    for k in range(1, count):
        peer = lax.rem(me + k, count)
        copy = pltpu.make_async_remote_copy(
            src_ref=src.at[peer],
            dst_ref=out.at[me],
            send_sem=send_sem.at[k],
            recv_sem=recv_sem.at[k],
            device_id={"chan": peer},
            device_id_type=pl.DeviceIdType.MESH,
        )
        copy.start()
        copies.append(copy)
    own.wait()
    for copy in copies:
        copy.wait()


def exchange(x):
    count = lax.axis_size("chan")
    return pl.pallas_call(
        functools.partial(exchange_body, count),
        in_specs=[pl.BlockSpec(memory_space=pl.ANY)],
        out_specs=pl.BlockSpec(memory_space=pl.ANY),
        out_shape=jax.ShapeDtypeStruct(x.shape, x.dtype),
        scratch_shapes=[
            pltpu.SemaphoreType.DMA((count,)),
            pltpu.SemaphoreType.DMA((count,)),
            pltpu.SemaphoreType.DMA,
        ],
        compiler_params=pltpu.CompilerParams(collective_id=0, has_side_effects=True),
        name="exchange",
    )(x)


def edges(slab):
    count = lax.axis_size("depth")
    up = lax.ppermute(slab[-1:], "depth", [(i, (i + 1) % count) for i in range(count)])
    down = lax.ppermute(slab[:1], "depth", [((i + 1) % count, i) for i in range(count)])
    return up, down


def per_device(volume, conv_weight, norm_gain, mlp_in, mlp_out):
    channels, planes, cells = volume.shape
    count = lax.axis_size("chan")
    chunk = planes * cells // count
    slab = jnp.swapaxes(volume, 0, 1)
    kernels = conv_weight[0]
    inner = conv(slab, *edges(slab), kernels[0])
    inner = conv(inner, *edges(inner), kernels[1])
    mixed = conv(inner, *edges(inner), kernels[2], slab, chunk)
    runs = exchange(mixed)
    done = mlp(runs.reshape(count * channels, chunk), norm_gain[0], mlp_in[0], mlp_out[0])
    back = exchange(done.reshape(count, channels, chunk))
    back = back.reshape(planes, cells // chunk, channels, chunk)
    return back.transpose(2, 0, 1, 3).reshape(volume.shape)


def solution(mesh):
    in_specs = (P("chan", "depth", None), P(None, None, "chan", None, None), P(), P(), P())
    out_specs = P("chan", "depth", None)
    return jax.shard_map(
        per_device, mesh=mesh, in_specs=in_specs, out_specs=out_specs, check_vma=False
    )
```

profile of v0, /device:TPU:9, one launch (start us, length us, event | category | flops | bytes accessed | tf_op | source)
XLA Modules:
  0.0 133.5 jit_solution(7699520841956990870)
XLA Ops:
  0.0 1.9 %copy.12 = f32[64,4,1024]{2,0,1:T(8,128)S(1)} copy(f32[64,4,1024]{2,1,0:T(4,128)} %param.5) | data formatting | bytes 2097152 | tf_op args[0]
  1.9 0.0 copy-start
  2.0 1.3 collective-permute-start
  3.2 1.2 collective-permute-start.1
  4.4 0.9 slice_bitcast_fusion
  5.3 4.8 %collective-permute-done.refs_1_ = f32[1,64,1024]{2,1,0:T(8,128)S(1)} collective-permute-done((f32[1,64,1024]{2,1,0:T(8,128)S(1)}, f32[1,64,1024]{2,1,0:T(8,128)S(1)}, u32[]{:S(2)}, u32[]{:S(2)}) %collective-permute-start) | collective-permute-done | bytes 262176 | tf_op jit(solution)/shard_map/ppermute | solution.py:203
  10.1 5.7 %collective-permute-done.1.refs_2_ = f32[1,64,1024]{2,1,0:T(8,128)S(1)} collective-permute-done((f32[1,64,1024]{2,1,0:T(8,128)S(1)}, f32[1,64,1024]{2,1,0:T(8,128)S(1)}, u32[]{:S(2)}, u32[]{:S(2)}) %collective-permute-start.1) | collective-permute-done | bytes 262176 | tf_op jit(solution)/shard_map/ppermute | solution.py:204
  15.8 0.0 copy-done.2
  15.8 0.7 copy-done.4
  16.5 7.1 %conv.3.refs_0_ = f32[4,64,1024]{2,1,0:T(8,128)} custom-call(f32[4,64,1024]{2,1,0:T(8,128)} %bitcast.18, f32[1,64,1024]{2,1,0:T(8,128)} %copy-done.2, f32[1,64,1024]{2,1,0:T(8,128)} %copy-done.4, f32[2,32,864]{2,1,0:T(8,128)} %get-tuple-element.12.refs_3_), custom_call_target="tpu_custom_call" | custom-call | tf_op jit(solution)/shard_map/conv/pallas_call | solution.py:100
  23.6 1.1 fusion.1
  24.7 0.0 copy-start.8
  24.7 1.3 collective-permute-start.2
  25.9 1.2 collective-permute-start.3
  27.1 4.9 %collective-permute-done.2.refs_1_ = f32[1,64,1024]{2,1,0:T(8,128)S(1)} collective-permute-done((f32[1,64,1024]{2,1,0:T(8,128)S(1)}, f32[1,64,1024]{2,1,0:T(8,128)S(1)}, u32[]{:S(2)}, u32[]{:S(2)}) %collective-permute-start.2) | collective-permute-done | bytes 262176 | tf_op jit(solution)/shard_map/ppermute | solution.py:203
  31.9 4.7 %collective-permute-done.3.refs_2_ = f32[1,64,1024]{2,1,0:T(8,128)S(1)} collective-permute-done((f32[1,64,1024]{2,1,0:T(8,128)S(1)}, f32[1,64,1024]{2,1,0:T(8,128)S(1)}, u32[]{:S(2)}, u32[]{:S(2)}) %collective-permute-start.3) | collective-permute-done | bytes 262176 | tf_op jit(solution)/shard_map/ppermute | solution.py:204
  36.6 0.7 copy-done.5
  37.3 7.1 %conv.4.refs_0_ = f32[4,64,1024]{2,1,0:T(8,128)} custom-call(f32[4,64,1024]{2,1,0:T(8,128)} %conv.3.refs_0_, f32[1,64,1024]{2,1,0:T(8,128)} %copy-done.3, f32[1,64,1024]{2,1,0:T(8,128)} %copy-done.5, f32[2,32,864]{2,1,0:T(8,128)} %get-tuple-element.13.refs_3_), custom_call_target="tpu_custom_call" | custom-call | tf_op jit(solution)/shard_map/conv/pallas_call | solution.py:100
  44.5 1.1 fusion
  45.5 1.2 collective-permute-start.4
  46.8 1.2 collective-permute-start.5
  48.0 0.0 copy-done.8
  48.0 0.9 copy.9.gain
  48.8 2.9 %collective-permute-done.4.refs_1_ = f32[1,64,1024]{2,1,0:T(8,128)S(1)} collective-permute-done((f32[1,64,1024]{2,1,0:T(8,128)S(1)}, f32[1,64,1024]{2,1,0:T(8,128)S(1)}, u32[]{:S(2)}, u32[]{:S(2)}) %collective-permute-start.4) | collective-permute-done | bytes 262176 | tf_op jit(solution)/shard_map/ppermute | solution.py:203
  51.7 5.9 %collective-permute-done.5.refs_2_ = f32[1,64,1024]{2,1,0:T(8,128)S(1)} collective-permute-done((f32[1,64,1024]{2,1,0:T(8,128)S(1)}, f32[1,64,1024]{2,1,0:T(8,128)S(1)}, u32[]{:S(2)}, u32[]{:S(2)}) %collective-permute-start.5) | collective-permute-done | bytes 262176 | tf_op jit(solution)/shard_map/ppermute | solution.py:204
  57.6 0.7 copy-done.7
  58.3 7.1 %conv.5.src = f32[8,64,512]{2,1,0:T(8,128)} custom-call(f32[4,64,1024]{2,1,0:T(8,128)} %conv.4.refs_0_, f32[1,64,1024]{2,1,0:T(8,128)} %copy-done.6, f32[1,64,1024]{2,1,0:T(8,128)} %copy-done.7, f32[4,64,1024]{2,1,0:T(8,128)} %bitcast.19, f32[2,32,864]{2,1,0:T(8,128)} %get-tuple-element.11.refs_4_), custom_call_target="tpu_custom_call" | custom-call | tf_op jit(solution)/shard_map/conv/pallas_call | solution.py:100
  65.5 29.5 %exchange.2 = f32[8,64,512]{2,1,0:T(8,128)} custom-call(f32[8,64,512]{2,1,0:T(8,128)} %conv.5.src), custom_call_target="tpu_custom_call" | custom-call | tf_op jit(solution)/shard_map/exchange/pallas_call | solution.py:186
  95.0 8.1 %mlp.1 = f32[512,512]{1,0:T(8,128)} custom-call(f32[512,512]{1,0:T(8,128)} %bitcast.20, f32[512,1]{1,0:T(8,128)} %copy.9.gain, f32[1024,512]{1,0:T(8,128)} %bitcast.23, f32[512,1024]{1,0:T(8,128)} %bitcast.24), custom_call_target="tpu_custom_call" | custom-call | tf_op jit(solution)/shard_map/mlp/pallas_call | solution.py:136
  103.1 26.3 %exchange.3 = f32[8,64,512]{2,1,0:T(8,128)} custom-call(f32[8,64,512]{2,1,0:T(8,128)} %bitcast.21), custom_call_target="tpu_custom_call" | custom-call | tf_op jit(solution)/shard_map/exchange/pallas_call | solution.py:186
  129.4 2.0 %copy.10 = f32[64,4,2,512]{3,2,1,0:T(2,128)S(1)} copy(f32[64,4,2,512]{3,0,2,1:T(8,128)} %bitcast.22) | data formatting | bytes 2097152 | tf_op jit(solution)/shard_map/transpose | solution.py:221
  131.4 2.0 %reshape.21 = f32[64,4,1024]{2,1,0:T(4,128)} reshape(f32[64,4,2,512]{3,2,1,0:T(2,128)S(1)} %copy.10) | data formatting | bytes 2097152 | tf_op jit(solution)/shard_map/reshape | solution.py:221
  (12 shorter events, 0.1 us)
Async XLA Ops:
  0.0 4.4 %copy-start.1 = (f32[1,3,2,32,864]{4,3,2,1,0:T(8,128)S(1)}, f32[1,3,2,32,864]{4,3,2,1,0:T(8,128)}, u32[]{:S(2)}) copy-start(f32[1,3,2,32,864]{4,3,2,1,0:T(8,128)} %param.6) | copy-start | bytes 1990660
  1.9 13.9 %copy-start = (f32[64,4,1024]{2,0,1:T(8,128)}, f32[64,4,1024]{2,0,1:T(8,128)S(1)}, u32[]{:S(2)}) copy-start(f32[64,4,1024]{2,0,1:T(8,128)S(1)} %copy.12) | copy-start | bytes 3145732
  2.0 8.1 %collective-permute-start = (f32[1,64,1024]{2,1,0:T(8,128)S(1)}, f32[1,64,1024]{2,1,0:T(8,128)S(1)}, u32[]{:S(2)}, u32[]{:S(2)}) collective-permute-start(f32[1,64,1024]{2,1,0:T(8,128)S(1)} %get-tuple-element.10), channel_id=1, source_target_pairs={{0,8},{8,16},{16,24},{24,0},{1,9},{9,17},{17,25},{25,1},{2,10},{10... | collective-permute-start | bytes 786440 | tf_op jit(solution)/shard_map/ppermute | solution.py:203
  3.2 12.6 %collective-permute-start.1 = (f32[1,64,1024]{2,1,0:T(8,128)S(1)}, f32[1,64,1024]{2,1,0:T(8,128)S(1)}, u32[]{:S(2)}, u32[]{:S(2)}) collective-permute-start(f32[1,64,1024]{2,1,0:T(8,128)S(1)} %get-tuple-element.9), channel_id=1, source_target_pairs={{8,0},{16,8},{24,16},{0,24},{9,1},{17,9},{25,17},{1,25},{10,2},{18... | collective-permute-start | bytes 786440 | tf_op jit(solution)/shard_map/ppermute | solution.py:204
  10.1 5.7 %copy-start.2 = (f32[1,64,1024]{2,1,0:T(8,128)}, f32[1,64,1024]{2,1,0:T(8,128)S(1)}, u32[]{:S(2)}) copy-start(f32[1,64,1024]{2,1,0:T(8,128)S(1)} %collective-permute-done.refs_1_) | copy-start | bytes 786436
  15.8 0.7 copy-start.4
  24.7 23.3 %copy-start.8 = (f32[1,512]{1,0:T(1,128)S(1)}, f32[1,512]{1,0:T(1,128)}, u32[]{:S(2)}) copy-start(f32[1,512]{1,0:T(1,128)} %param.7) | copy-start | bytes 6148
  24.7 7.3 %collective-permute-start.2 = (f32[1,64,1024]{2,1,0:T(8,128)S(1)}, f32[1,64,1024]{2,1,0:T(8,128)S(1)}, u32[]{:S(2)}, u32[]{:S(2)}) collective-permute-start(f32[1,64,1024]{2,1,0:T(8,128)S(1)} %get-tuple-element.8), channel_id=1, source_target_pairs={{0,8},{8,16},{16,24},{24,0},{1,9},{9,17},{17,25},{25,1},{2,10},{10... | collective-permute-start | bytes 786440 | tf_op jit(solution)/shard_map/ppermute | solution.py:203
  25.9 10.7 %collective-permute-start.3 = (f32[1,64,1024]{2,1,0:T(8,128)S(1)}, f32[1,64,1024]{2,1,0:T(8,128)S(1)}, u32[]{:S(2)}, u32[]{:S(2)}) collective-permute-start(f32[1,64,1024]{2,1,0:T(8,128)S(1)} %get-tuple-element.7), channel_id=1, source_target_pairs={{8,0},{16,8},{24,16},{0,24},{9,1},{17,9},{25,17},{1,25},{10,2},{18... | collective-permute-start | bytes 786440 | tf_op jit(solution)/shard_map/ppermute | solution.py:204
  31.9 4.7 %copy-start.3 = (f32[1,64,1024]{2,1,0:T(8,128)}, f32[1,64,1024]{2,1,0:T(8,128)S(1)}, u32[]{:S(2)}) copy-start(f32[1,64,1024]{2,1,0:T(8,128)S(1)} %collective-permute-done.2.refs_1_) | copy-start | bytes 786436
  36.6 0.7 copy-start.5
  45.5 6.2 %collective-permute-start.4 = (f32[1,64,1024]{2,1,0:T(8,128)S(1)}, f32[1,64,1024]{2,1,0:T(8,128)S(1)}, u32[]{:S(2)}, u32[]{:S(2)}) collective-permute-start(f32[1,64,1024]{2,1,0:T(8,128)S(1)} %get-tuple-element.6), channel_id=1, source_target_pairs={{0,8},{8,16},{16,24},{24,0},{1,9},{9,17},{17,25},{25,1},{2,10},{10... | collective-permute-start | bytes 786440 | tf_op jit(solution)/shard_map/ppermute | solution.py:203
  46.8 10.8 %collective-permute-start.5 = (f32[1,64,1024]{2,1,0:T(8,128)S(1)}, f32[1,64,1024]{2,1,0:T(8,128)S(1)}, u32[]{:S(2)}, u32[]{:S(2)}) collective-permute-start(f32[1,64,1024]{2,1,0:T(8,128)S(1)} %get-tuple-element.5), channel_id=1, source_target_pairs={{8,0},{16,8},{24,16},{0,24},{9,1},{17,9},{25,17},{1,25},{10,2},{18... | collective-permute-start | bytes 786440 | tf_op jit(solution)/shard_map/ppermute | solution.py:204
  51.7 5.9 %copy-start.6 = (f32[1,64,1024]{2,1,0:T(8,128)}, f32[1,64,1024]{2,1,0:T(8,128)S(1)}, u32[]{:S(2)}) copy-start(f32[1,64,1024]{2,1,0:T(8,128)S(1)} %collective-permute-done.4.refs_1_) | copy-start | bytes 786436
  57.6 0.7 copy-start.7
where the time goes:
time: 134 us; the launch traced here: 133 us
  Pallas kernels  85.3 us (64%)
  waiting for transfers between devices  28.8 us (21%)
  local copies, waits for them, and re-layouts  12.1 us (9%)
  starting transfers between devices  7.28 us (5%)
    pallas_call x2, Pallas kernels, exchange(): pl.pallas_call(functools.partial(exchange_body, count), in_specs=[pl.Bloc...  55.8 us
    pallas_call x3, Pallas kernels, conv(): pl.pallas_call(functools.partial(conv_body, last, chunk), grid=(groups,),...  21.4 us
    ppermute x3, waiting for transfers between devices, edges(): lax.ppermute(slab[:1], 'depth', [((i + 1) % count, i) for i in range(coun...  16.3 us
    ppermute x3, waiting for transfers between devices, edges(): lax.ppermute(slab[-1:], 'depth', [(i, (i + 1) % count) for i in range(cou...  12.5 us
    pallas_call x1, Pallas kernels, mlp(): pl.pallas_call(mlp_body, grid=(hid // block,), in_specs=[whole, pl.BlockS...  8.06 us
    unnamed x19, local copies, waits for them, and re-layouts  4.04 us
    ppermute x3, starting transfers between devices, edges(): lax.ppermute(slab[-1:], 'depth', [(i, (i + 1) % count) for i in range(cou...  3.77 us
    ppermute x3, starting transfers between devices, edges(): lax.ppermute(slab[:1], 'depth', [((i + 1) % count, i) for i in range(coun...  3.51 us
  transfers between devices with their start and end apart: 6, of which 6 were waited for; matrix products, arithmetic and copies ran while one was open for 1% of the time, Pallas kernels for 0%

commit v1 on v0

v1 whole, which is shorter than its diff:
```python
import functools

import jax
import jax.numpy as jnp
from jax import lax
from jax.experimental import pallas as pl
from jax.experimental.pallas import tpu as pltpu
from jax.sharding import PartitionSpec as P

W = 32
LANES = 128
LIMIT = 60 * 1024 * 1024
MESH = pl.DeviceIdType.MESH


def split(x):
    hi = x.astype(jnp.bfloat16)
    return hi, (x - hi.astype(jnp.float32)).astype(jnp.bfloat16)


def dot(a, b):
    return jnp.dot(a, b, preferred_element_type=jnp.float32)


def block_body(
    depth, chan, vin, wconv, gain, w_in, w_out, out,
    xs, xb, acc, wraw, wf, wmat, edge, halo, ybuf, rin, obuf,
    in_f, out_f, in_hi, in_lo, out_hi, out_lo, r_hi, r_lo, mo,
    x_recv, w_sem, halo_send, swap_send, edge_send, edge_recv,
    y_send, y_recv, o_send, o_recv,
):
    groups, planes, width, cells = vin.shape
    total = groups * planes
    teams = depth // groups
    tiles = cells // LANES
    rows = chan // tiles
    slots = planes // rows
    channels = groups * width
    part = 3 * width
    span = 3 * part

    d = lax.axis_index("depth")
    c = lax.axis_index("chan")
    j = lax.rem(d, groups)
    t = lax.div(d, groups)
    tile = lax.rem(c, tiles)
    row = lax.div(c, tiles)
    flip = j > 0
    above = lax.rem(t + 1, teams)
    below = lax.rem(t + teams - 1, teams)

    def place(q):
        return jnp.where(flip, total - 1 - q, q)

    barrier = pltpu.get_barrier_semaphore()
    peers = 0
    for team in (above, below) if teams > 2 else (above,):
        for k in range(groups):
            pl.semaphore_signal(barrier, inc=1, device_id={"depth": team * groups + k}, device_id_type=MESH)
            peers += 1
    for g in range(groups):
        for k in range(1 if g == 0 else 0, chan):
            pl.semaphore_signal(
                barrier, inc=1,
                device_id={"depth": t * groups + lax.rem(j + g, groups), "chan": lax.rem(c + k, chan)},
                device_id_type=MESH,
            )
            peers += 1

    loads = [pltpu.make_async_copy(wconv.at[0, l, j], wraw.at[l], w_sem.at[l]) for l in range(3)]
    for load in loads:
        load.start()
    for z in range(planes):
        slot = j * planes + z + 1
        pltpu.make_async_copy(vin.at[j, z], xs.at[slot], x_recv.at[slot]).start()
    in_load = pltpu.make_async_copy(w_in.at[0], in_f, w_sem.at[3])
    out_load = pltpu.make_async_copy(w_out.at[0], out_f, w_sem.at[4])
    in_load.start()
    out_load.start()

    pl.semaphore_wait(barrier, peers)

    def halo_copy(side, k):
        return pltpu.make_async_remote_copy(
            src_ref=vin.at[k, 0 if side == 0 else planes - 1],
            dst_ref=xs.at[total + 1 if side == 0 else 0],
            send_sem=halo_send.at[side, k],
            recv_sem=x_recv.at[total + 1 if side == 0 else 0],
            device_id={"depth": (below if side == 0 else above) * groups + k},
            device_id_type=MESH,
        )

    def swap_copy(k, i):
        peer = lax.rem(j + k, groups)
        z = jnp.where(peer == 0, i, planes - 1 - i)
        slot = j * planes + z + 1
        return pltpu.make_async_remote_copy(
            src_ref=vin.at[peer, z],
            dst_ref=xs.at[slot],
            send_sem=swap_send.at[k, i],
            recv_sem=x_recv.at[slot],
            device_id={"depth": t * groups + peer},
            device_id_type=MESH,
        )

    @pl.when(j == 0)
    def _():
        for k in reversed(range(groups)):
            halo_copy(0, k).start()

    @pl.when(j == groups - 1)
    def _():
        for k in range(groups):
            halo_copy(1, k).start()

    for i in range(planes):
        for k in range(1, groups):
            swap_copy(k, i).start()

    for l in range(3):
        loads[l].wait()
        for b in range(3):
            for e in range(3):
                for a in range(3):
                    start = ((b * 3 + e) * 3 + a) * width
                    piece = wraw[l, :, start : start + width]
                    hi = piece.astype(jnp.bfloat16).astype(jnp.float32)
                    for n, value in enumerate((hi, hi, piece - hi)):
                        col = ((a * 3 + n) * 3 + e) * width
                        wf[b * width : (b + 1) * width, col : col + width] = value
        wmat[l] = wf[...].astype(jnp.bfloat16)

    in_load.wait()
    out_load.wait()
    hidden = in_f.shape[0]
    step = 64

    def widen(k, _):
        at = pl.ds(pl.multiple_of(k * step, step), step)
        in_hi[at, :], in_lo[at, :] = split(in_f[at, :] * gain[...])
        return 0

    lax.fori_loop(0, hidden // step, widen, 0)

    def widen(k, _):
        at = pl.ds(pl.multiple_of(k * step, step), step)
        out_hi[at, :], out_lo[at, :] = split(out_f[at, :])
        return 0

    lax.fori_loop(0, out_f.shape[0] // step, widen, 0)

    column = lax.broadcasted_iota(jnp.int32, (width, cells), 1) % W

    def prepare(l, slot, x):
        before = jnp.where(column == 0, pltpu.roll(x, cells + 1 - W, 1), pltpu.roll(x, 1, 1))
        after = jnp.where(column == W - 1, pltpu.roll(x, W - 1, 1), pltpu.roll(x, cells - 1, 1))
        for e, value in enumerate((before, x, after)):
            hi, lo = split(value)
            for n, piece in enumerate((hi, lo, hi)):
                at = pl.multiple_of(slot * span + (n * 3 + e) * width, width)
                xb[l, pl.ds(at, width), :] = piece

    def conv(l, p):
        at = pl.ds(pl.multiple_of(p * span, width), 3 * span)
        for n in range(0, cells, 256):
            acc[:, n : n + 256] = dot(wmat[l], xb[l, at, n : n + 256])
        p0, p1, p2 = (acc[b * width : (b + 1) * width, :] for b in range(3))
        return p1 + pltpu.roll(p0, W, 1) + pltpu.roll(p2, cells - W, 1)

    def arrive(q):
        slot = place(q) + 1
        pltpu.make_async_copy(xs.at[slot], xs.at[slot], x_recv.at[slot]).wait()
        prepare(0, slot, xs[slot])

    def edge_copy(l, side):
        front = jnp.where(flip, above, below)
        back = jnp.where(flip, below, above)
        return pltpu.make_async_remote_copy(
            src_ref=edge.at[l, side],
            dst_ref=halo.at[l, 1 - side],
            send_sem=edge_send.at[l, side],
            recv_sem=edge_recv.at[l, 1 - side],
            device_id={"depth": (front if side == 0 else back) * groups + j},
            device_id_type=MESH,
        )

    def send_edge(l, side, u):
        edge[l, side] = u
        edge_copy(l, side).start()

    def take_halo(l, side):
        pltpu.make_async_copy(halo.at[l, side], halo.at[l, side], edge_recv.at[l, side]).wait()
        prepare(l + 1, place(-1 if side == 0 else total) + 1, halo[l, side])

    def inner(l, q):
        p = place(q)
        u = jax.nn.gelu(conv(l, p))
        prepare(l + 1, p + 1, u)
        return u

    def y_target(p, k):
        z = lax.rem(p, planes)
        m = lax.div(p, planes)
        at = lax.rem(tile + tiles // 2 + k, tiles)
        peer = lax.rem(z, rows) * tiles + at
        own = jnp.logical_and(m == j, peer == c)
        src = ybuf.at[p, :, pl.ds(pl.multiple_of(at * LANES, LANES), LANES)]
        slot = lax.div(z, rows)
        first = pl.multiple_of((c * groups + j) * width, width)
        dst = rin.at[slot, pl.ds(first, width), :]
        copy = pltpu.make_async_remote_copy(
            src_ref=src, dst_ref=dst, send_sem=y_send.at[p, k], recv_sem=y_recv.at[slot],
            device_id={"depth": t * groups + m, "chan": peer}, device_id_type=MESH,
        )
        return own, copy, src, dst, y_recv.at[slot]

    def outer(q):
        p = place(q)
        ybuf[p] = xs[p + 1] + conv(2, p)

        def send(k, _):
            own, copy, src, dst, sem = y_target(p, k)

            @pl.when(own)
            def _():
                pltpu.make_async_copy(src, dst, sem).start()

            @pl.when(jnp.logical_not(own))
            def _():
                copy.start()

            return 0

        lax.fori_loop(0, tiles, send, 0)

    arrive(-1)
    arrive(0)

    def wave(i, _):
        arrive(i + 1)
        u = inner(0, i)

        @pl.when(i == 0)
        def _():
            send_edge(0, 0, u)

        @pl.when(i == total - 1)
        def _():
            send_edge(0, 1, u)

        @pl.when(i >= 2)
        def _():
            inner(1, i - 1)

        @pl.when(i >= 4)
        def _():
            outer(i - 2)

        return 0

    lax.fori_loop(0, total, wave, 0)
    take_halo(0, 1)
    send_edge(1, 1, inner(1, total - 1))
    outer(total - 2)
    take_halo(0, 0)
    send_edge(1, 0, inner(1, 0))
    outer(1)
    take_halo(1, 0)
    outer(0)
    take_halo(1, 1)
    outer(total - 1)

    block = min(256, hidden)
    chunks = slots // 2

    def o_target(slot, k):
        peer = lax.rem(c + chan // 2 + k, chan)
        first = pl.multiple_of(peer * channels, channels)
        src = obuf.at[slot, pl.ds(first, channels), :]
        dst = out.at[slot * rows + row, :, pl.ds(pl.multiple_of(tile * LANES, LANES), LANES)]
        copy = pltpu.make_async_remote_copy(
            src_ref=src, dst_ref=dst, send_sem=o_send.at[slot, k], recv_sem=o_recv,
            device_id={"chan": peer}, device_id_type=MESH,
        )
        return peer == c, copy, src, dst

    def chunk(n, _):
        first = jnp.where(flip, n, chunks - 1 - n) * 2
        for s in range(2):
            pltpu.make_async_copy(rin.at[first + s], rin.at[first + s], y_recv.at[first + s]).wait()
            x = rin[first + s]
            r = x * lax.rsqrt(jnp.mean(x * x, axis=0, keepdims=True) + 1e-06)
            at = slice(s * LANES, (s + 1) * LANES)
            r_hi[:, at], r_lo[:, at] = split(r)
            mo[:, at] = x

        def mix(k, _):
            at = pl.ds(pl.multiple_of(k * block, block), block)
            h = dot(in_hi[at, :], r_hi[...]) + (dot(in_hi[at, :], r_lo[...]) + dot(in_lo[at, :], r_hi[...]))
            h_hi, h_lo = split(jax.nn.gelu(h))
            mo[...] += dot(out_hi[:, at], h_hi) + (dot(out_hi[:, at], h_lo) + dot(out_lo[:, at], h_hi))
            return 0

        lax.fori_loop(0, hidden // block, mix, 0)
        for s in range(2):
            obuf[first + s] = mo[:, s * LANES : (s + 1) * LANES]

            def send(k, _):
                own, copy, src, dst = o_target(first + s, k)

                @pl.when(own)
                def _():
                    pltpu.make_async_copy(src, dst, o_recv).start()

                @pl.when(jnp.logical_not(own))
                def _():
                    copy.start()

                return 0

            lax.fori_loop(0, chan, send, 0)
        return 0

    lax.fori_loop(0, chunks, chunk, 0)

    @pl.when(j == 0)
    def _():
        for k in range(groups):
            halo_copy(0, k).wait_send()

    @pl.when(j == groups - 1)
    def _():
        for k in range(groups):
            halo_copy(1, k).wait_send()

    for i in range(planes):
        for k in range(1, groups):
            swap_copy(k, i).wait_send()
    for l in range(2):
        for side in range(2):
            edge_copy(l, side).wait_send()

    def drain(n, _):
        own, copy, *_ = y_target(lax.div(n, tiles), lax.rem(n, tiles))

        @pl.when(jnp.logical_not(own))
        def _():
            copy.wait_send()

        return 0

    lax.fori_loop(0, total * tiles, drain, 0)

    def drain(n, _):
        own, copy, *_ = o_target(lax.div(n, chan), lax.rem(n, chan))

        @pl.when(jnp.logical_not(own))
        def _():
            copy.wait_send()

        return 0

    lax.fori_loop(0, slots * chan, drain, 0)
    pltpu.make_async_copy(out, out, o_recv).wait()


def per_device(volume, conv_weight, norm_gain, mlp_in, mlp_out):
    channels, planes, cells = volume.shape
    width, taps = conv_weight.shape[-2:]
    groups = channels // width
    depth, chan = lax.axis_size("depth"), lax.axis_size("chan")
    total = groups * planes
    tiles = cells // LANES
    slots = planes // (chan // tiles)
    hidden, every = mlp_in.shape[1:]
    vin = volume.reshape(groups, width, planes, cells).transpose(0, 2, 1, 3)
    f32, bf16 = jnp.float32, jnp.bfloat16
    dma = pltpu.SemaphoreType.DMA
    anywhere = pl.BlockSpec(memory_space=pl.ANY)
    out = pl.pallas_call(
        functools.partial(block_body, depth, chan),
        in_specs=[anywhere, anywhere, pl.BlockSpec(memory_space=pltpu.VMEM), anywhere, anywhere],
        out_specs=anywhere,
        out_shape=jax.ShapeDtypeStruct((planes, channels, cells), f32),
        scratch_shapes=[
            pltpu.VMEM((total + 2, width, cells), f32),
            pltpu.VMEM((3, (total + 2) * 9 * width, cells), bf16),
            pltpu.VMEM((3 * width, cells), f32),
            pltpu.VMEM((3, width, taps), f32),
            pltpu.VMEM((3 * width, 27 * width), f32),
            pltpu.VMEM((3, 3 * width, 27 * width), bf16),
            pltpu.VMEM((2, 2, width, cells), f32),
            pltpu.VMEM((2, 2, width, cells), f32),
            pltpu.VMEM((total, width, cells), f32),
            pltpu.VMEM((slots, every, LANES), f32),
            pltpu.VMEM((slots, every, LANES), f32),
            pltpu.VMEM((hidden, every), f32),
            pltpu.VMEM((every, hidden), f32),
            pltpu.VMEM((hidden, every), bf16),
            pltpu.VMEM((hidden, every), bf16),
            pltpu.VMEM((every, hidden), bf16),
            pltpu.VMEM((every, hidden), bf16),
            pltpu.VMEM((every, 2 * LANES), bf16),
            pltpu.VMEM((every, 2 * LANES), bf16),
            pltpu.VMEM((every, 2 * LANES), f32),
            dma((total + 2,)),
            dma((5,)),
            dma((2, groups)),
            dma((groups, planes)),
            dma((2, 2)),
            dma((2, 2)),
            dma((total, tiles)),
            dma((slots,)),
            dma((slots, chan)),
            dma,
        ],
        compiler_params=pltpu.CompilerParams(
            vmem_limit_bytes=LIMIT, collective_id=0, has_side_effects=True
        ),
        name="block",
    )(vin, conv_weight, norm_gain, mlp_in, mlp_out)
    return out.transpose(1, 0, 2)


def solution(mesh):
    in_specs = (P("chan", "depth", None), P(None, None, "chan", None, None), P(), P(), P())
    out_specs = P("chan", "depth", None)
    return jax.shard_map(
        per_device, mesh=mesh, in_specs=in_specs, out_specs=out_specs, check_vma=False
    )
```

time: 134 us -> 74.8 us (0.56)
  the two profiles are of different devices: /device:TPU:9 before, /device:TPU:0 now
where the time goes in v1:
time: 74.8 us; the launch traced here: 74.6 us
  Pallas kernels  68.9 us (92%)
  local copies, waits for them, and re-layouts  5.68 us (8%)
    pallas_call x1, Pallas kernels, per_device(): pl.pallas_call(functools.partial(block_body, depth, chan), in_specs=[anyw...  68.9 us
    transpose x1, local copies, waits for them, and re-layouts, per_device(): return out.transpose(1, 0, 2)  2.87 us
    reshape x1, local copies, waits for them, and re-layouts, per_device(): vin = volume.reshape(groups, width, planes, cells).transpose(0, 2, 1, 3)  2.8 us

profile of v1, /device:TPU:0, one launch (start us, length us, event | category | flops | bytes accessed | tf_op | source)
XLA Modules:
  0.0 74.6 jit_solution(2554298804026050647)
XLA Ops:
  0.0 2.8 %copy.13 = f32[2,32,4,1024]{3,1,2,0:T(8,128)} copy(f32[2,32,4,1024]{3,2,1,0:T(4,128)} %bitcast.7) | data formatting | bytes 2097152 | tf_op jit(solution)/shard_map/reshape | solution.py:376
  2.8 68.9 %block.1 = f32[4,64,1024]{2,1,0:T(8,128)} custom-call(f32[2,4,32,1024]{3,2,1,0:T(8,128)} %bitcast.6, f32[1,3,2,32,864]{4,3,2,1,0:T(8,128)} %wconv.1, f32[1,512]{1,0:T(1,128)} %gain.1, f32[1,1024,512]{2,1,0:T(8,128)} %w_in.1, f32[1,512,1024]{2,1,0:T(8,128)} %w_out.1), custom_call_target="tpu_custom_call" | custom-call | tf_op jit(solution)/shard_map/block/pallas_call | solution.py:380
  71.7 2.9 %copy.9 = f32[64,4,1024]{2,1,0:T(4,128)} copy(f32[64,4,1024]{2,0,1:T(8,128)} %bitcast.5) | data formatting | bytes 2097152 | tf_op jit(solution)/shard_map/transpose | solution.py:422

commit v2 on v1

--- a/solution.py
+++ b/solution.py
@@ -9,7 +9,7 @@
 
 W = 32
 LANES = 128
-LIMIT = 60 * 1024 * 1024
+LIMIT = 40 * 1024 * 1024
 MESH = pl.DeviceIdType.MESH
 
 
@@ -23,13 +23,13 @@
 
 
 def block_body(
-    depth, chan, vin, wconv, gain, w_in, w_out, out,
-    xs, xb, acc, wraw, wf, wmat, edge, halo, ybuf, rin, obuf,
-    in_f, out_f, in_hi, in_lo, out_hi, out_lo, r_hi, r_lo, mo,
-    x_recv, w_sem, halo_send, swap_send, edge_send, edge_recv,
+    depth, chan, groups, planes, raw, wconv, norm, w_in, w_out, out,
+    rows_in, vin, xs, xb, acc, wraw, wf, wmat, edge, halo, ybuf, rin, obuf,
+    gain, in_f, out_f, in_hi, in_lo, out_hi, out_lo, r_hi, r_lo, mo,
+    raw_sem, x_recv, w_sem, halo_send, swap_send, edge_send, edge_recv,
     y_send, y_recv, o_send, o_recv,
 ):
-    groups, planes, width, cells = vin.shape
+    width, cells = xs.shape[1:]
     total = groups * planes
     teams = depth // groups
     tiles = cells // LANES
@@ -51,6 +51,9 @@
 
     def place(q):
         return jnp.where(flip, total - 1 - q, q)
+
+    raw_load = pltpu.make_async_copy(raw, rows_in, raw_sem)
+    raw_load.start()
 
     barrier = pltpu.get_barrier_semaphore()
     peers = 0
@@ -70,14 +73,23 @@
     loads = [pltpu.make_async_copy(wconv.at[0, l, j], wraw.at[l], w_sem.at[l]) for l in range(3)]
     for load in loads:
         load.start()
+    in_load = pltpu.make_async_copy(w_in.at[0], in_f, w_sem.at[3])
+    out_load = pltpu.make_async_copy(w_out.at[0], out_f, w_sem.at[4])
+    gain_load = pltpu.make_async_copy(norm, gain, w_sem.at[5])
+    gain_load.start()
+    in_load.start()
+    out_load.start()
+
+    raw_load.wait()
+    pitch = tiles * planes
+    for k in range(groups):
+        for z in range(planes):
+            for n in range(tiles):
+                rows_at = pl.ds(k * width * pitch + n * planes + z, width, stride=pitch)
+                vin[k, z, :, n * LANES : (n + 1) * LANES] = rows_in[rows_at, :]
     for z in range(planes):
         slot = j * planes + z + 1
         pltpu.make_async_copy(vin.at[j, z], xs.at[slot], x_recv.at[slot]).start()
-    in_load = pltpu.make_async_copy(w_in.at[0], in_f, w_sem.at[3])
-    out_load = pltpu.make_async_copy(w_out.at[0], out_f, w_sem.at[4])
-    in_load.start()
-    out_load.start()
-
     pl.semaphore_wait(barrier, peers)
 
     def halo_copy(side, k):
@@ -130,6 +142,7 @@
                         wf[b * width : (b + 1) * width, col : col + width] = value
         wmat[l] = wf[...].astype(jnp.bfloat16)
 
+    gain_load.wait()
     in_load.wait()
     out_load.wait()
     hidden = in_f.shape[0]
@@ -277,7 +290,7 @@
         peer = lax.rem(c + chan // 2 + k, chan)
         first = pl.multiple_of(peer * channels, channels)
         src = obuf.at[slot, pl.ds(first, channels), :]
-        dst = out.at[slot * rows + row, :, pl.ds(pl.multiple_of(tile * LANES, LANES), LANES)]
+        dst = out.at[:, tile * planes + slot * rows + row, 0, :]
         copy = pltpu.make_async_remote_copy(
             src_ref=src, dst_ref=dst, send_sem=o_send.at[slot, k], recv_sem=o_recv,
             device_id={"chan": peer}, device_id_type=MESH,
@@ -373,16 +386,19 @@
     tiles = cells // LANES
     slots = planes // (chan // tiles)
     hidden, every = mlp_in.shape[1:]
-    vin = volume.reshape(groups, width, planes, cells).transpose(0, 2, 1, 3)
+    raw = volume.reshape(channels, planes, tiles, LANES).transpose(0, 2, 1, 3).reshape(-1, LANES)
     f32, bf16 = jnp.float32, jnp.bfloat16
     dma = pltpu.SemaphoreType.DMA
-    anywhere = pl.BlockSpec(memory_space=pl.ANY)
+    keep = functools.partial(pltpu.with_memory_space_constraint, memory_space=pltpu.HBM)
+    far = pl.BlockSpec(memory_space=pltpu.HBM)
     out = pl.pallas_call(
-        functools.partial(block_body, depth, chan),
-        in_specs=[anywhere, anywhere, pl.BlockSpec(memory_space=pltpu.VMEM), anywhere, anywhere],
-        out_specs=anywhere,
-        out_shape=jax.ShapeDtypeStruct((planes, channels, cells), f32),
+        functools.partial(block_body, depth, chan, groups, planes),
+        in_specs=[far] * 5,
+        out_specs=pl.BlockSpec(memory_space=pl.ANY),
+        out_shape=jax.ShapeDtypeStruct((channels, tiles * planes, 1, LANES), f32),
         scratch_shapes=[
+            pltpu.VMEM(raw.shape, f32),
+            pltpu.VMEM((groups, planes, width, cells), f32),
             pltpu.VMEM((total + 2, width, cells), f32),
             pltpu.VMEM((3, (total + 2) * 9 * width, cells), bf16),
             pltpu.VMEM((3 * width, cells), f32),
@@ -394,6 +410,7 @@
             pltpu.VMEM((total, width, cells), f32),
             pltpu.VMEM((slots, every, LANES), f32),
             pltpu.VMEM((slots, every, LANES), f32),
+            pltpu.VMEM((1, every), f32),
             pltpu.VMEM((hidden, every), f32),
             pltpu.VMEM((every, hidden), f32),
             pltpu.VMEM((hidden, every), bf16),
@@ -403,8 +420,9 @@
             pltpu.VMEM((every, 2 * LANES), bf16),
             pltpu.VMEM((every, 2 * LANES), bf16),
             pltpu.VMEM((every, 2 * LANES), f32),
+            dma,
             dma((total + 2,)),
-            dma((5,)),
+            dma((6,)),
             dma((2, groups)),
             dma((groups, planes)),
             dma((2, 2)),
@@ -418,8 +436,9 @@
             vmem_limit_bytes=LIMIT, collective_id=0, has_side_effects=True
         ),
         name="block",
-    )(vin, conv_weight, norm_gain, mlp_in, mlp_out)
-    return out.transpose(1, 0, 2)
+    )(keep(raw), keep(conv_weight), keep(norm_gain), keep(mlp_in), keep(mlp_out))
+    out = out.reshape(channels, tiles, planes, LANES).transpose(0, 2, 1, 3)
+    return out.reshape(volume.shape)
 
 
 def solution(mesh):

time: 74.8 us -> 68.5 us (0.916)
  local copies, waits for them, and re-layouts: 5.68 us -> 0.97 us
  Pallas kernels: 68.9 us -> 67.3 us
    transpose x1 -> x0, local copies, waits for them, and re-layouts: 2.87 us -> none  [per_device(): return out.transpose(1, 0, 2)]
    reshape x1 -> x0, local copies, waits for them, and re-layouts: 2.8 us -> none  [per_device(): vin = volume.reshape(groups, width, planes, cells).transpose(0, 2, 1, 3)]
    pallas_call x1, Pallas kernels: 68.9 us -> 67.3 us  [per_device(): pl.pallas_call(functools.partial(block_body, depth, chan, groups, planes)...]
    unnamed x0 -> x1, local copies, waits for them, and re-layouts: none -> 0.97 us
where the time goes in v2:
time: 68.5 us; the launch traced here: 68.3 us
  Pallas kernels  67.3 us (98%)
  local copies, waits for them, and re-layouts  0.97 us (1%)
    pallas_call x1, Pallas kernels, per_device(): pl.pallas_call(functools.partial(block_body, depth, chan, groups, planes)...  67.3 us

profile of v2, /device:TPU:0, one launch (start us, length us, event | category | flops | bytes accessed | tf_op | source)
XLA Modules:
  0.0 68.3 jit_solution(8190432008191363384)
XLA Ops:
  0.0 67.3 %block.1 = f32[64,32,1,128]{3,2,1,0:T(1,128)S(1)} custom-call(f32[2048,128]{1,0:T(8,128)} %bitcast.11, f32[1,3,2,32,864]{4,3,2,1,0:T(8,128)} %wconv.1, f32[1,512]{1,0:T(1,128)} %norm.1, f32[1,1024,512]{2,1,0:T(8,128)} %w_in.1, f32[1,512,1024]{2,1,0:T(8,128)} %w_out.1), custom_call_target="tpu_custom_call" | custom-call | tf_op jit(solution)/shard_map/block/pallas_call | solution.py:394
  67.4 1.0 %copy.9 = f32[64,4,1024]{2,1,0:T(4,128)} copy(f32[64,4,1024]{2,1,0:T(4,128)S(1)} %bitcast.10) | data formatting | bytes 2097152

commit v3 on v2

--- a/solution.py
+++ b/solution.py
@@ -80,18 +80,6 @@
     in_load.start()
     out_load.start()
 
-    raw_load.wait()
-    pitch = tiles * planes
-    for k in range(groups):
-        for z in range(planes):
-            for n in range(tiles):
-                rows_at = pl.ds(k * width * pitch + n * planes + z, width, stride=pitch)
-                vin[k, z, :, n * LANES : (n + 1) * LANES] = rows_in[rows_at, :]
-    for z in range(planes):
-        slot = j * planes + z + 1
-        pltpu.make_async_copy(vin.at[j, z], xs.at[slot], x_recv.at[slot]).start()
-    pl.semaphore_wait(barrier, peers)
-
     def halo_copy(side, k):
         return pltpu.make_async_remote_copy(
             src_ref=vin.at[k, 0 if side == 0 else planes - 1],
@@ -102,9 +90,12 @@
             device_id_type=MESH,
         )
 
+    def swap_plane(k, i):
+        peer = lax.rem(j + k, groups)
+        return peer, jnp.where(peer == 0, i, planes - 1 - i)
+
     def swap_copy(k, i):
-        peer = lax.rem(j + k, groups)
-        z = jnp.where(peer == 0, i, planes - 1 - i)
+        peer, z = swap_plane(k, i)
         slot = j * planes + z + 1
         return pltpu.make_async_remote_copy(
             src_ref=vin.at[peer, z],
@@ -115,19 +106,53 @@
             device_id_type=MESH,
         )
 
-    @pl.when(j == 0)
-    def _():
-        for k in reversed(range(groups)):
-            halo_copy(0, k).start()
-
-    @pl.when(j == groups - 1)
-    def _():
+    pitch = tiles * planes
+
+    def fetch(k, z):
+        for n in range(tiles):
+            at = pl.ds(k * width * pitch + n * planes + z, width, stride=pitch)
+            vin[k, z, :, n * LANES : (n + 1) * LANES] = rows_in[at, :]
+
+    def halo_start(low, high):
+        @pl.when(j == 0)
+        def _():
+            for k in low:
+                halo_copy(0, k).start()
+
+        @pl.when(j == groups - 1)
+        def _():
+            for k in high:
+                halo_copy(1, k).start()
+
+    def keep(z):
+        slot = j * planes + z + 1
+        pltpu.make_async_copy(vin.at[j, z], xs.at[slot], x_recv.at[slot]).start()
+
+    raw_load.wait()
+    if groups == 2:
+        other = 1 - j
+        fetch(other, jnp.where(j == 0, 0, planes - 1))
+        pl.semaphore_wait(barrier, peers)
+        halo_start([1], [0])
+        for i in range(planes):
+            if i < planes - 1:
+                fetch(*swap_plane(1, i))
+            swap_copy(1, i).start()
+        for z in range(planes):
+            fetch(j, z)
+            keep(z)
+        halo_start([0], [1])
+    else:
         for k in range(groups):
-            halo_copy(1, k).start()
-
-    for i in range(planes):
-        for k in range(1, groups):
-            swap_copy(k, i).start()
+            for z in range(planes):
+                fetch(k, z)
+        pl.semaphore_wait(barrier, peers)
+        halo_start(range(groups), range(groups))
+        for i in range(planes):
+            for k in range(1, groups):
+                swap_copy(k, i).start()
+        for z in range(planes):
+            keep(z)
 
     for l in range(3):
         loads[l].wait()
@@ -141,26 +166,6 @@
                         col = ((a * 3 + n) * 3 + e) * width
                         wf[b * width : (b + 1) * width, col : col + width] = value
         wmat[l] = wf[...].astype(jnp.bfloat16)
-
-    gain_load.wait()
-    in_load.wait()
-    out_load.wait()
-    hidden = in_f.shape[0]
-    step = 64
-
-    def widen(k, _):
-        at = pl.ds(pl.multiple_of(k * step, step), step)
-        in_hi[at, :], in_lo[at, :] = split(in_f[at, :] * gain[...])
-        return 0
-
-    lax.fori_loop(0, hidden // step, widen, 0)
-
-    def widen(k, _):
-        at = pl.ds(pl.multiple_of(k * step, step), step)
-        out_hi[at, :], out_lo[at, :] = split(out_f[at, :])
-        return 0
-
-    lax.fori_loop(0, out_f.shape[0] // step, widen, 0)
 
     column = lax.broadcasted_iota(jnp.int32, (width, cells), 1) % W
 
@@ -246,24 +251,33 @@
 
         lax.fori_loop(0, tiles, send, 0)
 
+    def own(q, _):
+        arrive(q)
+        return 0
+
+    def first(q, _):
+        inner(0, q)
+        return 0
+
+    def second(q, _):
+        inner(1, q)
+        return 0
+
+    lax.fori_loop(0, planes, own, 0)
+    lax.fori_loop(1, planes - 1, first, 0)
     arrive(-1)
-    arrive(0)
+    send_edge(0, 0, inner(0, 0))
+    lax.fori_loop(1, planes - 2, second, 0)
 
     def wave(i, _):
         arrive(i + 1)
         u = inner(0, i)
 
-        @pl.when(i == 0)
-        def _():
-            send_edge(0, 0, u)
-
         @pl.when(i == total - 1)
         def _():
             send_edge(0, 1, u)
 
-        @pl.when(i >= 2)
-        def _():
-            inner(1, i - 1)
+        inner(1, i - 1)
 
         @pl.when(i >= 4)
         def _():
@@ -271,10 +285,30 @@
 
         return 0
 
-    lax.fori_loop(0, total, wave, 0)
+    lax.fori_loop(planes - 1, total, wave, 0)
     take_halo(0, 1)
     send_edge(1, 1, inner(1, total - 1))
     outer(total - 2)
+    gain_load.wait()
+    in_load.wait()
+    out_load.wait()
+    hidden = in_f.shape[0]
+    step = 64
+
+    def widen(k, _):
+        at = pl.ds(pl.multiple_of(k * step, step), step)
+        in_hi[at, :], in_lo[at, :] = split(in_f[at, :] * gain[...])
+        return 0
+
+    lax.fori_loop(0, hidden // step, widen, 0)
+
+    def widen(k, _):
+        at = pl.ds(pl.multiple_of(k * step, step), step)
+        out_hi[at, :], out_lo[at, :] = split(out_f[at, :])
+        return 0
+
+    lax.fori_loop(0, out_f.shape[0] // step, widen, 0)
+
     take_halo(0, 0)
     send_edge(1, 0, inner(1, 0))
     outer(1)

time: 68.5 us -> 66.6 us (0.972)
  Pallas kernels: 67.3 us -> 65.5 us
    pallas_call x1, Pallas kernels: 67.3 us -> 65.5 us  [per_device(): pl.pallas_call(functools.partial(block_body, depth, chan, groups, planes)...]
where the time goes in v3:
time: 66.6 us; the launch traced here: 66.4 us
  Pallas kernels  65.5 us (98%)
  local copies, waits for them, and re-layouts  0.97 us (1%)
    pallas_call x1, Pallas kernels, per_device(): pl.pallas_call(functools.partial(block_body, depth, chan, groups, planes)...  65.5 us

profile of v3, /device:TPU:0, one launch (start us, length us, event | category | flops | bytes accessed | tf_op | source)
XLA Modules:
  0.0 66.4 jit_solution(3079880724846417761)
XLA Ops:
  0.0 65.5 %block.1 = f32[64,32,1,128]{3,2,1,0:T(1,128)S(1)} custom-call(f32[2048,128]{1,0:T(8,128)} %bitcast.11, f32[1,3,2,32,864]{4,3,2,1,0:T(8,128)} %wconv.1, f32[1,512]{1,0:T(1,128)} %norm.1, f32[1,1024,512]{2,1,0:T(8,128)} %w_in.1, f32[1,512,1024]{2,1,0:T(8,128)} %w_out.1), custom_call_target="tpu_custom_call" | custom-call | tf_op jit(solution)/shard_map/block/pallas_call | solution.py:428
  65.5 1.0 %copy.9 = f32[64,4,1024]{2,1,0:T(4,128)} copy(f32[64,4,1024]{2,1,0:T(4,128)S(1)} %bitcast.10) | data formatting | bytes 2097152

commit v4 on v3

--- a/solution.py
+++ b/solution.py
@@ -130,14 +130,13 @@
 
     raw_load.wait()
     if groups == 2:
-        other = 1 - j
-        fetch(other, jnp.where(j == 0, 0, planes - 1))
+        fetch(*swap_plane(1, 0))
         pl.semaphore_wait(barrier, peers)
-        halo_start([1], [0])
         for i in range(planes):
-            if i < planes - 1:
+            if i > 0:
                 fetch(*swap_plane(1, i))
             swap_copy(1, i).start()
+        halo_start([1], [0])
         for z in range(planes):
             fetch(j, z)
             keep(z)
@@ -259,16 +258,8 @@
         inner(0, q)
         return 0
 
-    def second(q, _):
-        inner(1, q)
-        return 0
-
     lax.fori_loop(0, planes, own, 0)
     lax.fori_loop(1, planes - 1, first, 0)
-    arrive(-1)
-    send_edge(0, 0, inner(0, 0))
-    lax.fori_loop(1, planes - 2, second, 0)
-
     def wave(i, _):
         arrive(i + 1)
         u = inner(0, i)
@@ -279,16 +270,21 @@
 
         inner(1, i - 1)
 
-        @pl.when(i >= 4)
+        @pl.when(i >= 5)
         def _():
             outer(i - 2)
 
         return 0
 
     lax.fori_loop(planes - 1, total, wave, 0)
-    take_halo(0, 1)
-    send_edge(1, 1, inner(1, total - 1))
-    outer(total - 2)
+    arrive(-1)
+    send_edge(0, 0, inner(0, 0))
+    inner(1, 1)
+    if total > 4:
+        outer(2)
+    take_halo(0, 0)
+    send_edge(1, 0, inner(1, 0))
+    outer(1)
     gain_load.wait()
     in_load.wait()
     out_load.wait()
@@ -309,13 +305,13 @@
 
     lax.fori_loop(0, out_f.shape[0] // step, widen, 0)
 
-    take_halo(0, 0)
-    send_edge(1, 0, inner(1, 0))
-    outer(1)
+    take_halo(0, 1)
+    send_edge(1, 1, inner(1, total - 1))
+    outer(total - 2)
+    take_halo(1, 1)
+    outer(total - 1)
     take_halo(1, 0)
     outer(0)
-    take_halo(1, 1)
-    outer(total - 1)
 
     block = min(256, hidden)
     chunks = slots // 2

time: 66.6 us -> 66.4 us (level)
  no operation moved by 1% of the time
where the time goes in v4:
time: 66.4 us; the launch traced here: 66.2 us
  Pallas kernels  65.3 us (98%)
  local copies, waits for them, and re-layouts  0.97 us (1%)
    pallas_call x1, Pallas kernels, per_device(): pl.pallas_call(functools.partial(block_body, depth, chan, groups, planes)...  65.3 us

profile of v4, /device:TPU:0, one launch (start us, length us, event | category | flops | bytes accessed | tf_op | source)
XLA Modules:
  0.0 66.2 jit_solution(4466305196917415615)
XLA Ops:
  0.0 65.3 %block.1 = f32[64,32,1,128]{3,2,1,0:T(1,128)S(1)} custom-call(f32[2048,128]{1,0:T(8,128)} %bitcast.11, f32[1,3,2,32,864]{4,3,2,1,0:T(8,128)} %wconv.1, f32[1,512]{1,0:T(1,128)} %norm.1, f32[1,1024,512]{2,1,0:T(8,128)} %w_in.1, f32[1,512,1024]{2,1,0:T(8,128)} %w_out.1), custom_call_target="tpu_custom_call" | custom-call | tf_op jit(solution)/shard_map/block/pallas_call | solution.py:424
  65.3 1.0 %copy.9 = f32[64,4,1024]{2,1,0:T(4,128)} copy(f32[64,4,1024]{2,1,0:T(4,128)S(1)} %bitcast.10) | data formatting | bytes 2097152

commit v5 on v4

--- a/solution.py
+++ b/solution.py
@@ -166,16 +166,22 @@
                         wf[b * width : (b + 1) * width, col : col + width] = value
         wmat[l] = wf[...].astype(jnp.bfloat16)
 
-    column = lax.broadcasted_iota(jnp.int32, (width, cells), 1) % W
+
+    lane = lax.broadcasted_iota(jnp.int32, (width, LANES), 1)
+    left = jnp.where(lane % W == 0, lane + W - 1, lane - 1)
+    right = jnp.where(lane % W == W - 1, lane - W + 1, lane + 1)
 
     def prepare(l, slot, x):
-        before = jnp.where(column == 0, pltpu.roll(x, cells + 1 - W, 1), pltpu.roll(x, 1, 1))
-        after = jnp.where(column == W - 1, pltpu.roll(x, W - 1, 1), pltpu.roll(x, cells - 1, 1))
-        for e, value in enumerate((before, x, after)):
-            hi, lo = split(value)
-            for n, piece in enumerate((hi, lo, hi)):
-                at = pl.multiple_of(slot * span + (n * 3 + e) * width, width)
-                xb[l, pl.ds(at, width), :] = piece
+        for n in range(tiles):
+            at_n = slice(n * LANES, (n + 1) * LANES)
+            piece = x[:, at_n]
+            before = jnp.take_along_axis(piece, left, axis=1, mode="promise_in_bounds")
+            after = jnp.take_along_axis(piece, right, axis=1, mode="promise_in_bounds")
+            for e, value in enumerate((before, piece, after)):
+                hi, lo = split(value)
+                for m, kept in enumerate((hi, lo, hi)):
+                    at = pl.multiple_of(slot * span + (m * 3 + e) * width, width)
+                    xb[l, pl.ds(at, width), at_n] = kept
 
     def conv(l, p):
         at = pl.ds(pl.multiple_of(p * span, width), 3 * span)

time: 66.4 us -> 66.5 us (level)
  no operation moved by 1% of the time
where the time goes in v5:
time: 66.5 us; the launch traced here: 66.3 us
  Pallas kernels  65.3 us (98%)
  local copies, waits for them, and re-layouts  0.97 us (1%)
    pallas_call x1, Pallas kernels, per_device(): pl.pallas_call(functools.partial(block_body, depth, chan, groups, planes)...  65.3 us

profile of v5, /device:TPU:0, one launch (start us, length us, event | category | flops | bytes accessed | tf_op | source)
XLA Modules:
  0.0 66.3 jit_solution(11870837740423082605)
XLA Ops:
  0.0 65.3 %block.1 = f32[64,32,1,128]{3,2,1,0:T(1,128)S(1)} custom-call(f32[2048,128]{1,0:T(8,128)} %bitcast.11, f32[1,3,2,32,864]{4,3,2,1,0:T(8,128)} %wconv.1, f32[1,512]{1,0:T(1,128)} %norm.1, f32[1,1024,512]{2,1,0:T(8,128)} %w_in.1, f32[1,512,1024]{2,1,0:T(8,128)} %w_out.1), custom_call_target="tpu_custom_call" | custom-call | tf_op jit(solution)/shard_map/block/pallas_call | solution.py:430
  65.3 1.0 %copy.9 = f32[64,4,1024]{2,1,0:T(4,128)} copy(f32[64,4,1024]{2,1,0:T(4,128)S(1)} %bitcast.10) | data formatting | bytes 2097152
